TPU v7x, 32 devices: a whole 2x2x4 slice. The times are simulated.
32 devices in a mesh: cluster: 16 (over z, x, core), blk: 2 (over y).
Axes of the slice: x: 2, y: 2, z: 4, core: 2. Of those that a mesh axis runs over, the one named last changes fastest.
Arguments:
- coeff: bfloat16 [512, 8, 2048], P('cluster', None, 'blk'), may hold values from -0.375 to 0.375
- intersection: int32 [16, 32], replicated, may hold values from 0 to 511, as said below
- basis_vals: bfloat16 [8192, 256], P(('cluster', 'blk')), may hold values from -6 to 6
- coulomb: bfloat16 [8192, 7, 256], P(('cluster', 'blk')), may hold values from -0.125 to 0.125
- reach: int32 [32], P(('cluster', 'blk')), may hold values from 0 to 3, as said below
Outputs:
- exchange_out: bfloat16 [8192, 2048], P(('cluster', 'blk'))
Inputs may be any that keep to these rules, and one draw needn't show every extreme that they name: `intersection`: each row lists 32 distinct atoms; atom a is owned by cluster a // 32; at most 4 atoms of one row have the same owner, and each row c holds exactly 4 atoms owned by cluster c. `reach`: some block reaches 3 and some block reaches 0.
All inputs are finite; a program needn't handle non-finite values.
Results may differ from a plain program's by a relative error of at most 0.0059.
Values may be sent and summed in bfloat16 or wider, within the bound.
No kernel may reach another device: no remote copies, remote signals or barrier semaphores. Data moves between devices by JAX's collectives and lax.ppermute only.
A program may use at most 64 MiB of HBM per device.

v0:
```python
import jax
import jax.numpy as jnp
from jax import lax
from jax.sharding import PartitionSpec as P


def passed_along(value, axis, steps):
    count = lax.axis_size(axis)
    pairs = [(source, (source + steps) % count) for source in range(count)]
    return lax.ppermute(value, axis, pairs)


def block_term(local_vals, source, coul_tile, within, norm_factor):
    density = (
        lax.dot_general(
            local_vals, source, (((1,), (1,)), ((), ())), preferred_element_type=jnp.float32
        )
        * norm_factor
    )
    masked_tile = jnp.where(
        within, density * coul_tile.astype(jnp.float32), jnp.float32(0.0)
    ).astype(jnp.bfloat16)
    return jnp.dot(masked_tile, source, preferred_element_type=jnp.float32)


def on_device(coeff, intersection, basis_vals, coulomb, reach):
    num_clusters = lax.axis_size("cluster")
    my_cluster = lax.axis_index("cluster")
    atom_count = coeff.shape[0]
    list_len = intersection.shape[1]
    capacity = 2 * list_len // num_clusters
    num_funcs = coeff.shape[1]
    my_columns = coeff.shape[2]
    half_stops = (coulomb.shape[1] - 1) // 2
    owners = intersection // atom_count
    same_owner = owners[:, :, None] == owners[:, None, :]
    earlier = jnp.arange(list_len)[None, :] < jnp.arange(list_len)[:, None]
    slot_rank = jnp.sum(jnp.logical_and(same_owner, earlier[None, :, :]).astype(jnp.int32), axis=2)
    matches = jnp.logical_and(
        (owners == my_cluster)[:, :, None],
        slot_rank[:, :, None] == jnp.arange(capacity)[None, None, :],
    )
    local_atom = intersection - my_cluster * atom_count
    source_rows = jnp.sum(jnp.where(matches, local_atom[:, :, None], 0), axis=1)
    filled = jnp.any(matches, axis=1)
    outgoing = jnp.take(coeff, source_rows.reshape(-1), axis=0)
    outgoing = jnp.where(filled.reshape(-1)[:, None, None], outgoing, jnp.zeros_like(outgoing))
    outgoing = outgoing.reshape(num_clusters, capacity, num_funcs, my_columns)
    incoming = lax.all_to_all(outgoing, "cluster", split_axis=0, concat_axis=0, tiled=True)
    my_owners = lax.dynamic_index_in_dim(owners, my_cluster, 0, keepdims=False)
    my_ranks = lax.dynamic_index_in_dim(slot_rank, my_cluster, 0, keepdims=False)
    positions = my_owners * capacity + my_ranks
    needed = jnp.take(
        incoming.reshape(num_clusters * capacity, num_funcs * my_columns), positions, axis=0
    )
    needed = needed.reshape(list_len * num_funcs, my_columns)
    all_columns = lax.all_gather(needed, "blk", axis=1, tiled=True)

    def convert(values):
        return jnp.dot(values, all_columns, preferred_element_type=jnp.float32).astype(jnp.bfloat16)

    local_vals = convert(basis_vals)
    norm_factor = local_vals.shape[1] ** (-0.5)
    my_reach = reach[0]

    def term(source, offset):
        return block_term(
            local_vals,
            source,
            coulomb[:, offset + half_stops, :],
            abs(offset) <= my_reach,
            norm_factor,
        )

    accumulated = term(local_vals, 0)
    upward = basis_vals
    downward = basis_vals
    for stop_num in range(1, half_stops + 1):
        upward = passed_along(upward, "blk", -1)
        accumulated = accumulated + term(convert(upward), stop_num)
        downward = passed_along(downward, "blk", 1)
        accumulated = accumulated + term(convert(downward), -stop_num)
    return accumulated.astype(jnp.bfloat16)


def solution(mesh):
    return jax.shard_map(
        on_device,
        mesh=mesh,
        in_specs=(
            P("cluster", None, "blk"),
            P(),
            P(("cluster", "blk"), None),
            P(("cluster", "blk"), None, None),
            P(("cluster", "blk")),
        ),
        out_specs=P(("cluster", "blk"), None),
        check_vma=False,
    )
```

profile of v0, /device:TPU:9, one launch (start us, length us, event | category | flops | bytes accessed | tf_op | source)
XLA Modules:
  0.0 91.6 jit_solution(14014058126347180299)
XLA Ops:
  6.5 0.8 broadcast_compare_fusion
  7.3 0.7 broadcast_subtract_fusion
  8.0 0.5 convert_reduce_fusion
  8.7 0.2 fusion.54
  9.2 0.6 gather_fusion
  9.8 1.2 %select_select_fusion = bf16[16,4,8,1024]{3,2,1,0:T(8,128)(2,1)} fusion(bf16[16,4,8,1024]{3,2,1,0:T(8,128)(2,1)S(1)} %bitcast.82, pred[16,4]{1,0:T(8,128)(4,1)S(1)} %copy.7, pred[16,4]{1,0:T(8,128)(4,1)S(1)} %copy.6), kind=kLoop, calls=%fused_computation.21 | loop fusion | flops 1048576 | bytes 2097280 | tf_op jit(solution)/shard_map/jit(_where)/select_n | solution.py:47
  11.0 6.5 %all-to-all-start = ((bf16[16,4,8,1024]{3,2,1,0:T(8,128)(2,1)}), bf16[16,4,8,1024]{3,2,1,0:T(8,128)(2,1)S(1)}, u32[]{:S(2)}, u32[]{:S(2)}) async-start(bf16[16,4,8,1024]{3,2,1,0:T(8,128)(2,1)} %select_select_fusion), calls=%async_computation | async-start | bytes 2097152 | tf_op jit(solution)/shard_map/all_to_all | solution.py:49
  17.8 24.7 %all-to-all-done = bf16[16,4,8,1024]{3,2,1,0:T(8,128)(2,1)S(1)} async-done(((bf16[16,4,8,1024]{3,2,1,0:T(8,128)(2,1)}), bf16[16,4,8,1024]{3,2,1,0:T(8,128)(2,1)S(1)}, u32[]{:S(2)}, u32[]{:S(2)}) %all-to-all-start) | async-done | bytes 1048608 | tf_op jit(solution)/shard_map/all_to_all | solution.py:49
  42.5 0.6 copy.9
  43.1 0.9 gather_fusion.1
  44.0 0.2 gather.15
  44.2 0.9 broadcast_select_fusion
  45.2 1.3 %collective-permute-start = (bf16[256,256]{1,0:T(8,128)(2,1)S(1)}, bf16[256,256]{1,0:T(8,128)(2,1)S(1)}, u32[]{:S(2)}, u32[]{:S(2)}) collective-permute-start(bf16[256,256]{1,0:T(8,128)(2,1)S(1)} %copy-done.5), channel_id=1, source_target_pairs={{0,1},{1,0},{2,3},{3,2},{4,5},{5,4},{6,7},{7,6},{8,9},{9,8},{10,11... | collective-permute-start | bytes 393224 | tf_op jit(solution)/shard_map/ppermute | solution.py:10
  46.5 4.3 %collective-permute-done = bf16[256,256]{1,0:T(8,128)(2,1)S(1)} collective-permute-done((bf16[256,256]{1,0:T(8,128)(2,1)S(1)}, bf16[256,256]{1,0:T(8,128)(2,1)S(1)}, u32[]{:S(2)}, u32[]{:S(2)}) %collective-permute-start) | collective-permute-done | bytes 131104 | tf_op jit(solution)/shard_map/ppermute | solution.py:10
  50.7 1.2 %collective-permute-start.1 = (bf16[256,256]{1,0:T(8,128)(2,1)S(1)}, bf16[256,256]{1,0:T(8,128)(2,1)S(1)}, u32[]{:S(2)}, u32[]{:S(2)}) collective-permute-start(bf16[256,256]{1,0:T(8,128)(2,1)S(1)} %collective-permute-done), channel_id=1, source_target_pairs={{0,1},{1,0},{2,3},{3,2},{4,5},{5,4},{6,7},{7,6},{8,9},{9,8},{10,11... | collective-permute-start | bytes 393224 | tf_op jit(solution)/shard_map/ppermute | solution.py:10
  52.7 4.1 %collective-permute-done.1 = bf16[256,256]{1,0:T(8,128)(2,1)S(1)} collective-permute-done((bf16[256,256]{1,0:T(8,128)(2,1)S(1)}, bf16[256,256]{1,0:T(8,128)(2,1)S(1)}, u32[]{:S(2)}, u32[]{:S(2)}) %collective-permute-start.1) | collective-permute-done | bytes 131104 | tf_op jit(solution)/shard_map/ppermute | solution.py:10
  56.7 2.3 %collective-permute-start.2 = (bf16[256,256]{1,0:T(8,128)(2,1)S(1)}, bf16[256,256]{1,0:T(8,128)(2,1)S(1)}, u32[]{:S(2)}, u32[]{:S(2)}) collective-permute-start(bf16[256,256]{1,0:T(8,128)(2,1)S(1)} %collective-permute-done.1), channel_id=1, source_target_pairs={{0,1},{1,0},{2,3},{3,2},{4,5},{5,4},{6,7},{7,6},{8,9},{9,8},{10,11... | collective-permute-start | bytes 393224 | tf_op jit(solution)/shard_map/ppermute | solution.py:10
  59.0 11.4 %all-gather.2.cloned.1.call-done = bf16[256,2048]{1,0:T(8,128)(2,1)} async-done(((bf16[256,1024]{1,0:T(8,128)(2,1)}), bf16[256,2048]{1,0:T(8,128)(2,1)}) %all-gather.2.cloned.1.call-update) | async-done | bytes 1048592 | tf_op jit(solution)/shard_map/all_gather | solution.py:57
  70.4 1.8 %convolution_convert_fusion.2 = bf16[2048,256]{1,0:T(8,128)(2,1)S(1)} fusion(bf16[256,2048]{1,0:T(8,128)(2,1)} %all-gather.2.cloned.1.call-done, bf16[256,256]{1,0:T(8,128)(2,1)S(1)} %collective-permute-done), kind=kOutput, calls=%fused_computation.11 | convolution fusion | flops 268959744 | bytes 2228224 | tf_op jit(solution)/shard_map/dot_general | solution.py:60
  72.2 0.5 convolution_convert_fusion.3
  72.7 0.5 convolution_multiply_fusion.2
  73.2 3.6 %fusion.4 = f32[256,2048]{1,0:T(8,128)} fusion(bf16[2048,256]{1,0:T(8,128)(2,1)S(1)} %convolution_convert_fusion.3, bf16[256,7,256]{2,0,1:T(8,128)(2,1)} %param.8, pred[]{:T(512)} %bitcast), kind=kOutput, calls=%fused_computation.20 | convolution fusion | flops 537198592 | bytes 5374464 | tf_op jit(solution)/shard_map/dot_general | solution.py:23
  76.8 2.6 %convolution_add_fusion.5 = f32[256,2048]{1,0:T(8,128)S(1)} fusion(f32[256,2048]{1,0:T(8,128)} %fusion.4, bf16[2048,256]{1,0:T(8,128)(2,1)} %copy-done.2, f32[256,256]{1,0:T(8,128)S(1)} %convolution_multiply_fusion.2, bf16[256,7,256]{2,0,1:T(8,128)(2,1)} %param.8, pred[]{:T(512)} %bitcast.7), kind=kOutput, calls=%fused_computation.7 | convolution fusion | flops 269221888 | bytes 5636608 | tf_op jit(solution)/shard_map/dot_general | solution.py:23
  79.4 0.5 convolution_add_fusion.4
  79.8 0.5 convolution_convert_fusion.1
  80.3 0.5 convolution_multiply_fusion.1
  80.8 0.5 convolution_add_fusion.3
  81.3 0.5 convolution_add_fusion.2
  81.8 0.5 convolution_convert_fusion
  82.3 0.5 convolution_multiply_fusion
  82.8 0.5 convolution_add_fusion.1
  83.3 1.4 %fusion = bf16[256,2048]{1,0:T(8,128)(2,1)} fusion(f32[256,2048]{1,0:T(8,128)S(1)} %convolution_add_fusion.1, bf16[2048,256]{1,0:T(8,128)(2,1)S(1)} %convolution_convert_fusion, f32[256,256]{1,0:T(8,128)S(1)} %convolution_multiply_fusion, bf16[256,7,256]{2,0,1:T(8,128)(2,1)S(1)} %copy-done.4, pred[]{:T(512)} %bitcast.13), kind=kOutput, calls=%fused_computation.8 | convolution fusion | flops 269746176 | bytes 4587521 | tf_op jit(solution)/shard_map/dot_general | solution.py:23
  (29 shorter events, 0.8 us)
Async XLA Ops:
  6.5 2.7 %copy-start = (bf16[32,8,1024]{2,1,0:T(8,128)(2,1)S(1)}, bf16[32,8,1024]{2,1,0:T(8,128)(2,1)}, u32[]{:S(2)}) copy-start(bf16[32,8,1024]{2,1,0:T(8,128)(2,1)} %param.5) | copy-start | bytes 1572868
  11.0 31.5 %all-to-all-start = ((bf16[16,4,8,1024]{3,2,1,0:T(8,128)(2,1)}), bf16[16,4,8,1024]{3,2,1,0:T(8,128)(2,1)S(1)}, u32[]{:S(2)}, u32[]{:S(2)}) async-start(bf16[16,4,8,1024]{3,2,1,0:T(8,128)(2,1)} %select_select_fusion), calls=%async_computation | async-start | bytes 2097152 | tf_op jit(solution)/shard_map/all_to_all | solution.py:49
  17.6 52.8 %all-gather.2.cloned.1.call-start = ((), (), s32[]{:S(2)}) async-start(), calls=%async_computation.1 | async-start | bytes 1572864 | tf_op jit(solution)/shard_map/all_gather | solution.py:57
  44.0 1.2 %copy-start.5 = (bf16[256,256]{1,0:T(8,128)(2,1)S(1)}, bf16[256,256]{1,0:T(8,128)(2,1)}, u32[]{:S(2)}) copy-start(bf16[256,256]{1,0:T(8,128)(2,1)} %param.7) | copy-start | bytes 393220
  45.2 5.6 %collective-permute-start = (bf16[256,256]{1,0:T(8,128)(2,1)S(1)}, bf16[256,256]{1,0:T(8,128)(2,1)S(1)}, u32[]{:S(2)}, u32[]{:S(2)}) collective-permute-start(bf16[256,256]{1,0:T(8,128)(2,1)S(1)} %copy-done.5), channel_id=1, source_target_pairs={{0,1},{1,0},{2,3},{3,2},{4,5},{5,4},{6,7},{7,6},{8,9},{9,8},{10,11... | collective-permute-start | bytes 393224 | tf_op jit(solution)/shard_map/ppermute | solution.py:10
  50.7 6.0 %collective-permute-start.1 = (bf16[256,256]{1,0:T(8,128)(2,1)S(1)}, bf16[256,256]{1,0:T(8,128)(2,1)S(1)}, u32[]{:S(2)}, u32[]{:S(2)}) collective-permute-start(bf16[256,256]{1,0:T(8,128)(2,1)S(1)} %collective-permute-done), channel_id=1, source_target_pairs={{0,1},{1,0},{2,3},{3,2},{4,5},{5,4},{6,7},{7,6},{8,9},{9,8},{10,11... | collective-permute-start | bytes 393224 | tf_op jit(solution)/shard_map/ppermute | solution.py:10
  56.7 25.1 %collective-permute-start.2 = (bf16[256,256]{1,0:T(8,128)(2,1)S(1)}, bf16[256,256]{1,0:T(8,128)(2,1)S(1)}, u32[]{:S(2)}, u32[]{:S(2)}) collective-permute-start(bf16[256,256]{1,0:T(8,128)(2,1)S(1)} %collective-permute-done.1), channel_id=1, source_target_pairs={{0,1},{1,0},{2,3},{3,2},{4,5},{5,4},{6,7},{7,6},{8,9},{9,8},{10,11... | collective-permute-start | bytes 393224 | tf_op jit(solution)/shard_map/ppermute | solution.py:10
  70.4 1.8 %copy-start.1 = (bf16[256,2048]{1,0:T(8,128)(2,1)S(1)}, bf16[256,2048]{1,0:T(8,128)(2,1)}, u32[]{:S(2)}) copy-start(bf16[256,2048]{1,0:T(8,128)(2,1)} %all-gather.2.cloned.1.call-done) | copy-start | bytes 3145732
  72.2 1.0 %copy-start.2 = (bf16[2048,256]{1,0:T(8,128)(2,1)}, bf16[2048,256]{1,0:T(8,128)(2,1)S(1)}, u32[]{:S(2)}) copy-start(bf16[2048,256]{1,0:T(8,128)(2,1)S(1)} %convolution_convert_fusion.2) | copy-start | bytes 3145732
  76.8 2.6 %copy-start.3 = (bf16[2048,256]{1,0:T(8,128)(2,1)S(1)}, bf16[2048,256]{1,0:T(8,128)(2,1)}, u32[]{:S(2)}) copy-start(bf16[2048,256]{1,0:T(8,128)(2,1)} %copy-done.2) | copy-start | bytes 3145732
  76.8 2.6 %copy-start.4 = (bf16[256,7,256]{2,0,1:T(8,128)(2,1)S(1)}, bf16[256,7,256]{2,0,1:T(8,128)(2,1)}, u32[]{:S(2)}) copy-start(bf16[256,7,256]{2,0,1:T(8,128)(2,1)} %param.8) | copy-start | bytes 2752516
Sparse Core Ops, SparseCore 0:
  45.3 25.0 all-gather.1
where the time goes:
time: 91.9 us; the launch traced here: 91.6 us
  waiting for transfers between devices  44.4 us (48%)
  between operations  14.3 us (16%)
  matrix products  14.2 us (15%)
  starting transfers between devices  11.4 us (12%)
  other arithmetic  4.38 us (5%)
  local copies, waits for them, and re-layouts  2.91 us (3%)
    all_to_all x1, waiting for transfers between devices, on_device(): lax.all_to_all(outgoing, 'cluster', split_axis=0, concat_axis=0, tiled=True)  24.7 us
    all_gather x1, waiting for transfers between devices, on_device(): all_columns = lax.all_gather(needed, 'blk', axis=1, tiled=True)  11.4 us
    dot_general x7, matrix products, block_term(): return jnp.dot(masked_tile, source, preferred_element_type=jnp.float32)  9.46 us
    ppermute x3, waiting for transfers between devices, passed_along(): return lax.ppermute(value, axis, pairs)  8.35 us
    all_to_all x1, starting transfers between devices, on_device(): lax.all_to_all(outgoing, 'cluster', split_axis=0, concat_axis=0, tiled=True)  6.55 us
    ppermute x3, starting transfers between devices, passed_along(): return lax.ppermute(value, axis, pairs)  4.85 us
    dot_general x4, matrix products, convert(): jnp.dot(values, all_columns, preferred_element_type=jnp.float32)  3.26 us
  transfers between devices with their start and end apart: 5, of which 4 were waited for; matrix products, arithmetic and copies ran while one was open for 13% of the time, Pallas kernels for 0%

commit v1 on v0

--- a/solution.py
+++ b/solution.py
@@ -2,6 +2,28 @@
 import jax.numpy as jnp
 from jax import lax
 from jax.sharding import PartitionSpec as P
+
+
+def in_order(blocks, dim):
+    lengths = list(blocks.shape[1:])
+    lengths[dim] *= blocks.shape[0]
+    return jnp.moveaxis(blocks, 0, dim).reshape(lengths)
+
+
+def collected_by_bits(x, axis):
+    peers = lax.axis_size(axis)
+    parts = x[None]
+    for level in range(peers.bit_length() - 1):
+        apart = 1 << level
+        other = lax.ppermute(parts, axis, [(i, i ^ apart) for i in range(peers)])
+        both = jnp.stack([parts, other])
+        upper = lax.axis_index(axis) >> level & 1
+        parts = jnp.where(upper == 0, both, both[::-1]).reshape(-1, *x.shape)
+    return parts
+
+
+def doubled_up(x, axis, dim):
+    return in_order(collected_by_bits(x, axis), dim)
 
 
 def passed_along(value, axis, steps):
@@ -54,7 +76,7 @@
         incoming.reshape(num_clusters * capacity, num_funcs * my_columns), positions, axis=0
     )
     needed = needed.reshape(list_len * num_funcs, my_columns)
-    all_columns = lax.all_gather(needed, "blk", axis=1, tiled=True)
+    all_columns = doubled_up(needed, "blk", 1)
 
     def convert(values):
         return jnp.dot(values, all_columns, preferred_element_type=jnp.float32).astype(jnp.bfloat16)

time: 91.9 us -> 76.5 us (0.83)
  between operations: 14.3 us -> 0.92 us
  waiting for transfers between devices: 44.4 us -> 42.7 us
  local copies, waits for them, and re-layouts: 2.91 us -> 4.51 us
  matrix products: 14.2 us -> 12.7 us
    all_gather x1 -> x0, waiting for transfers between devices: 11.4 us -> none  [on_device(): all_columns = lax.all_gather(needed, 'blk', axis=1, tiled=True)]
    ppermute x3, waiting for transfers between devices: 8.35 us -> 18 us  [passed_along(): return lax.ppermute(value, axis, pairs)]
    ppermute x3, starting transfers between devices: 4.85 us -> 2.79 us  [passed_along(): return lax.ppermute(value, axis, pairs)]
    dot_general x4, matrix products: 3.26 us -> 1.85 us  [convert(): jnp.dot(values, all_columns, preferred_element_type=jnp.float32)]
    ppermute x0 -> x1, starting transfers between devices: none -> 1.3 us  [collected_by_bits(): other = lax.ppermute(parts, axis, [(i, i ^ apart) for i in range(peers)])]
    unnamed x13 -> x11, local copies, waits for them, and re-layouts: 0.63 us -> 1.58 us
  transfers between devices with their start and end apart: 5 -> 5, of which waited for: 4 -> 3; matrix products, arithmetic and copies ran while one was open for 13% -> 14% of each run, Pallas kernels for 0% -> 0%
where the time goes in v1:
time: 76.5 us; the launch traced here: 75.3 us
  waiting for transfers between devices  42.7 us (56%)
  matrix products  12.7 us (17%)
  starting transfers between devices  10.6 us (14%)
  local copies, waits for them, and re-layouts  4.51 us (6%)
  other arithmetic  3.86 us (5%)
  between operations  0.92 us (1%)
    all_to_all x1, waiting for transfers between devices, on_device(): lax.all_to_all(outgoing, 'cluster', split_axis=0, concat_axis=0, tiled=True)  24.7 us
    ppermute x3, waiting for transfers between devices, passed_along(): return lax.ppermute(value, axis, pairs)  18 us
    dot_general x7, matrix products, block_term(): return jnp.dot(masked_tile, source, preferred_element_type=jnp.float32)  9.44 us
    all_to_all x1, starting transfers between devices, on_device(): lax.all_to_all(outgoing, 'cluster', split_axis=0, concat_axis=0, tiled=True)  6.55 us
    ppermute x3, starting transfers between devices, passed_along(): return lax.ppermute(value, axis, pairs)  2.79 us
    dot_general x4, matrix products, convert(): jnp.dot(values, all_columns, preferred_element_type=jnp.float32)  1.85 us
    gather x5, local copies, waits for them, and re-layouts, on_device(): jnp.take(incoming.reshape(num_clusters * capacity, num_funcs * my_columns...  1.77 us
    unnamed x11, local copies, waits for them, and re-layouts  1.58 us
  transfers between devices with their start and end apart: 5, of which 3 were waited for; matrix products, arithmetic and copies ran while one was open for 14% of the time, Pallas kernels for 0%

profile of v1, /device:TPU:9, one launch (start us, length us, event | category | flops | bytes accessed | tf_op | source)
XLA Modules:
  0.0 75.3 jit_solution(730649786990359814)
XLA Ops:
  0.0 0.8 %broadcast_compare_fusion = (pred[16,32]{1,0:T(8,128)(4,1)S(1)}, s32[16,32]{1,0:T(8,128)S(1)}) fusion(s32[]{:T(128)S(6)} %axis_index.25, s32[16,32]{1,0:T(8,128)} %param.6), kind=kLoop, calls=%fused_computation.91 | loop fusion | flops 8192 | bytes 4612 | tf_op jit(solution)/shard_map/eq | solution.py:62
  0.8 0.7 broadcast_subtract_fusion
  1.5 0.5 convert_reduce_fusion
  2.7 0.6 gather_fusion
  3.3 1.2 %select_select_fusion = bf16[16,4,8,1024]{3,2,1,0:T(8,128)(2,1)} fusion(bf16[16,4,8,1024]{3,2,1,0:T(8,128)(2,1)S(1)} %bitcast.92, pred[16,4]{1,0:T(8,128)(4,1)S(1)} %copy.9, pred[16,4]{1,0:T(8,128)(4,1)S(1)} %copy.8), kind=kLoop, calls=%fused_computation.23 | loop fusion | flops 1048576 | bytes 2097280 | tf_op jit(solution)/shard_map/jit(_where)/select_n | solution.py:69
  4.5 6.5 %all-to-all-start = ((bf16[16,4,8,1024]{3,2,1,0:T(8,128)(2,1)}), bf16[16,4,8,1024]{3,2,1,0:T(8,128)(2,1)S(1)}, u32[]{:S(2)}, u32[]{:S(2)}) async-start(bf16[16,4,8,1024]{3,2,1,0:T(8,128)(2,1)} %select_select_fusion), calls=%async_computation | async-start | bytes 2097152 | tf_op jit(solution)/shard_map/all_to_all | solution.py:71
  11.2 24.7 %all-to-all-done = bf16[16,4,8,1024]{3,2,1,0:T(8,128)(2,1)S(1)} async-done(((bf16[16,4,8,1024]{3,2,1,0:T(8,128)(2,1)}), bf16[16,4,8,1024]{3,2,1,0:T(8,128)(2,1)S(1)}, u32[]{:S(2)}, u32[]{:S(2)}) %all-to-all-start) | async-done | bytes 1048608 | tf_op jit(solution)/shard_map/all_to_all | solution.py:71
  35.9 0.6 copy.13
  36.5 0.9 %gather_fusion.1 = bf16[32,8192]{1,0:T(8,128)(2,1)S(1)} fusion(bf16[64,8192]{1,0:T(8,128)(2,1)S(1)} %bitcast.91, s32[1024]{0:T(1024)S(1)} %pad_clamp_fusion), kind=kCustom, calls=%fused_computation.1 | custom fusion | bytes 1048704 | tf_op jit(solution)/shard_map/jit(_take)/gather | solution.py:75
  37.4 0.2 gather.18
  38.0 1.3 %collective-permute-start = (bf16[1,256,1024]{1,2,0:T(8,128)(2,1)S(1)}, bf16[1,256,1024]{1,2,0:T(8,128)(2,1)S(1)}, u32[]{:S(2)}, u32[]{:S(2)}) collective-permute-start(bf16[1,256,1024]{1,2,0:T(8,128)(2,1)S(1)} %broadcast_select_fusion), channel_id=1, source_target_pairs={{0,1},{1,0},{2,3},{3,2},{4,5},{5,4},{6,7},{7,6},{8,9},{9,8},{10,11... | collective-permute-start | bytes 1572872 | tf_op jit(solution)/shard_map/ppermute | solution.py:18
  39.3 0.3 collective-permute-start.1
  39.6 15.2 %collective-permute-done.1 = bf16[256,256]{1,0:T(8,128)(2,1)S(1)} collective-permute-done((bf16[256,256]{1,0:T(8,128)(2,1)S(1)}, bf16[256,256]{1,0:T(8,128)(2,1)S(1)}, u32[]{:S(2)}, u32[]{:S(2)}) %collective-permute-start.1) | collective-permute-done | bytes 131104 | tf_op jit(solution)/shard_map/ppermute | solution.py:32
  54.8 1.2 %collective-permute-start.2 = (bf16[256,256]{1,0:T(8,128)(2,1)S(1)}, bf16[256,256]{1,0:T(8,128)(2,1)S(1)}, u32[]{:S(2)}, u32[]{:S(2)}) collective-permute-start(bf16[256,256]{1,0:T(8,128)(2,1)S(1)} %collective-permute-done.1), channel_id=1, source_target_pairs={{0,1},{1,0},{2,3},{3,2},{4,5},{5,4},{6,7},{7,6},{8,9},{9,8},{10,11... | collective-permute-start | bytes 393224 | tf_op jit(solution)/shard_map/ppermute | solution.py:32
  56.7 2.8 %collective-permute-done.2 = bf16[256,256]{1,0:T(8,128)(2,1)S(1)} collective-permute-done((bf16[256,256]{1,0:T(8,128)(2,1)S(1)}, bf16[256,256]{1,0:T(8,128)(2,1)S(1)}, u32[]{:S(2)}, u32[]{:S(2)}) %collective-permute-start.2) | collective-permute-done | bytes 131104 | tf_op jit(solution)/shard_map/ppermute | solution.py:32
  59.4 1.2 %collective-permute-start.3 = (bf16[256,256]{1,0:T(8,128)(2,1)S(1)}, bf16[256,256]{1,0:T(8,128)(2,1)S(1)}, u32[]{:S(2)}, u32[]{:S(2)}) collective-permute-start(bf16[256,256]{1,0:T(8,128)(2,1)S(1)} %collective-permute-done.2), channel_id=1, source_target_pairs={{0,1},{1,0},{2,3},{3,2},{4,5},{5,4},{6,7},{7,6},{8,9},{9,8},{10,11... | collective-permute-start | bytes 393224 | tf_op jit(solution)/shard_map/ppermute | solution.py:32
  60.7 0.2 gather.17
  61.5 0.5 convolution_convert_fusion.3
  62.0 0.5 convolution_convert_fusion.2
  62.5 1.0 %copy-done.1 = bf16[2048,256]{1,0:T(8,128)(2,1)} copy-done((bf16[2048,256]{1,0:T(8,128)(2,1)}, bf16[2048,256]{1,0:T(8,128)(2,1)S(1)}, u32[]{:S(2)}) %copy-start.1) | copy-done | bytes 1048600
  63.4 0.5 convolution_multiply_fusion.2
  63.9 3.5 %fusion.4 = f32[256,2048]{1,0:T(8,128)} fusion(bf16[2048,256]{1,0:T(8,128)(2,1)S(1)} %convolution_convert_fusion.3, bf16[256,7,256]{2,0,1:T(8,128)(2,1)} %param.8, pred[]{:T(512)} %bitcast), kind=kOutput, calls=%fused_computation.21 | convolution fusion | flops 537198592 | bytes 5374464 | tf_op jit(solution)/shard_map/dot_general | solution.py:45
  67.4 2.6 %convolution_add_fusion.5 = f32[256,2048]{1,0:T(8,128)S(1)} fusion(f32[256,2048]{1,0:T(8,128)} %fusion.4, bf16[2048,256]{1,0:T(8,128)(2,1)} %copy-done.1, f32[256,256]{1,0:T(8,128)S(1)} %convolution_multiply_fusion.2, bf16[256,7,256]{2,0,1:T(8,128)(2,1)} %param.8, pred[]{:T(512)} %bitcast.11), kind=kOutput, calls=%fused_computation.7 | convolution fusion | flops 269221888 | bytes 5636608 | tf_op jit(solution)/shard_map/dot_general | solution.py:45
  70.0 0.5 convolution_add_fusion.4
  70.5 0.5 convolution_convert_fusion.1
  71.0 0.5 convolution_multiply_fusion.1
  71.5 0.5 convolution_add_fusion.3
  71.9 0.5 convolution_add_fusion.2
  72.4 0.5 convolution_convert_fusion
  72.9 0.5 convolution_multiply_fusion
  73.4 0.5 convolution_add_fusion.1
  73.9 1.4 %fusion = bf16[256,2048]{1,0:T(8,128)(2,1)} fusion(f32[256,2048]{1,0:T(8,128)S(1)} %convolution_add_fusion.1, bf16[2048,256]{1,0:T(8,128)(2,1)S(1)} %convolution_convert_fusion, f32[256,256]{1,0:T(8,128)S(1)} %convolution_multiply_fusion, bf16[256,7,256]{2,0,1:T(8,128)(2,1)S(1)} %copy-done.3, pred[]{:T(512)} %bitcast.19), kind=kOutput, calls=%fused_computation.8 | convolution fusion | flops 269746176 | bytes 4587521 | tf_op jit(solution)/shard_map/dot_general | solution.py:45
  (32 shorter events, 1.7 us)
Async XLA Ops:
  0.0 2.7 %copy-start = (bf16[32,8,1024]{2,1,0:T(8,128)(2,1)S(1)}, bf16[32,8,1024]{2,1,0:T(8,128)(2,1)}, u32[]{:S(2)}) copy-start(bf16[32,8,1024]{2,1,0:T(8,128)(2,1)} %param.5) | copy-start | bytes 1572868
  4.5 31.5 %all-to-all-start = ((bf16[16,4,8,1024]{3,2,1,0:T(8,128)(2,1)}), bf16[16,4,8,1024]{3,2,1,0:T(8,128)(2,1)S(1)}, u32[]{:S(2)}, u32[]{:S(2)}) async-start(bf16[16,4,8,1024]{3,2,1,0:T(8,128)(2,1)} %select_select_fusion), calls=%async_computation | async-start | bytes 2097152 | tf_op jit(solution)/shard_map/all_to_all | solution.py:71
  37.4 1.8 %copy-start.4 = (bf16[256,256]{1,0:T(8,128)(2,1)S(1)}, bf16[256,256]{1,0:T(8,128)(2,1)}, u32[]{:S(2)}) copy-start(bf16[256,256]{1,0:T(8,128)(2,1)} %param.7) | copy-start | bytes 393220
  38.0 23.2 %collective-permute-start = (bf16[1,256,1024]{1,2,0:T(8,128)(2,1)S(1)}, bf16[1,256,1024]{1,2,0:T(8,128)(2,1)S(1)}, u32[]{:S(2)}, u32[]{:S(2)}) collective-permute-start(bf16[1,256,1024]{1,2,0:T(8,128)(2,1)S(1)} %broadcast_select_fusion), channel_id=1, source_target_pairs={{0,1},{1,0},{2,3},{3,2},{4,5},{5,4},{6,7},{7,6},{8,9},{9,8},{10,11... | collective-permute-start | bytes 1572872 | tf_op jit(solution)/shard_map/ppermute | solution.py:18
  39.3 15.5 %collective-permute-start.1 = (bf16[256,256]{1,0:T(8,128)(2,1)S(1)}, bf16[256,256]{1,0:T(8,128)(2,1)S(1)}, u32[]{:S(2)}, u32[]{:S(2)}) collective-permute-start(bf16[256,256]{1,0:T(8,128)(2,1)S(1)} %copy-done.4), channel_id=1, source_target_pairs={{0,1},{1,0},{2,3},{3,2},{4,5},{5,4},{6,7},{7,6},{8,9},{9,8},{10,11... | collective-permute-start | bytes 393224 | tf_op jit(solution)/shard_map/ppermute | solution.py:32
  54.8 4.7 %collective-permute-start.2 = (bf16[256,256]{1,0:T(8,128)(2,1)S(1)}, bf16[256,256]{1,0:T(8,128)(2,1)S(1)}, u32[]{:S(2)}, u32[]{:S(2)}) collective-permute-start(bf16[256,256]{1,0:T(8,128)(2,1)S(1)} %collective-permute-done.1), channel_id=1, source_target_pairs={{0,1},{1,0},{2,3},{3,2},{4,5},{5,4},{6,7},{7,6},{8,9},{9,8},{10,11... | collective-permute-start | bytes 393224 | tf_op jit(solution)/shard_map/ppermute | solution.py:32
  59.4 13.0 %collective-permute-start.3 = (bf16[256,256]{1,0:T(8,128)(2,1)S(1)}, bf16[256,256]{1,0:T(8,128)(2,1)S(1)}, u32[]{:S(2)}, u32[]{:S(2)}) collective-permute-start(bf16[256,256]{1,0:T(8,128)(2,1)S(1)} %collective-permute-done.2), channel_id=1, source_target_pairs={{0,1},{1,0},{2,3},{3,2},{4,5},{5,4},{6,7},{7,6},{8,9},{9,8},{10,11... | collective-permute-start | bytes 393224 | tf_op jit(solution)/shard_map/ppermute | solution.py:32
  62.4 1.0 %copy-start.1 = (bf16[2048,256]{1,0:T(8,128)(2,1)}, bf16[2048,256]{1,0:T(8,128)(2,1)S(1)}, u32[]{:S(2)}) copy-start(bf16[2048,256]{1,0:T(8,128)(2,1)S(1)} %convolution_convert_fusion.2) | copy-start | bytes 3145732
  67.4 2.6 %copy-start.2 = (bf16[2048,256]{1,0:T(8,128)(2,1)S(1)}, bf16[2048,256]{1,0:T(8,128)(2,1)}, u32[]{:S(2)}) copy-start(bf16[2048,256]{1,0:T(8,128)(2,1)} %copy-done.1) | copy-start | bytes 3145732
  67.4 2.6 %copy-start.3 = (bf16[256,7,256]{2,0,1:T(8,128)(2,1)S(1)}, bf16[256,7,256]{2,0,1:T(8,128)(2,1)}, u32[]{:S(2)}) copy-start(bf16[256,7,256]{2,0,1:T(8,128)(2,1)} %param.8) | copy-start | bytes 2752516
